TPU v7x, 32 devices: a whole 2x2x4 slice. The times are simulated.
32 devices in a mesh: dp: 8 (over z, x), latent: 4 (over y, core).
Axes of the slice: x: 2, y: 2, z: 4, core: 2. Of those that a mesh axis runs over, the one named last changes fastest.
Arguments:
- tokens: bfloat16 [1024, 1536], P('dp'), may hold values from -6 to 6
- enc_weight: bfloat16 [1536, 32768], P(None, ('dp', 'latent')), may hold values from -0.15625 to 0.15625
- enc_bias: float32 [32768], P(('dp', 'latent')), may hold values from -3 to 3
- dec_weight: bfloat16 [32768, 1536], P(('dp', 'latent')), may hold values from -0.0625 to 0.0625
- dec_bias: float32 [1536], replicated, may hold values from -3 to 3
- slot_token: int32 [1024], P(('dp', 'latent')), may hold values from 0 to 7
- slot_latent: int32 [1024], P(('dp', 'latent')), may hold values from 0 to 7
- slot_count: int32 [32], P(('dp', 'latent')), may hold values from 6 to 32, as said below
Outputs:
- enc_grad: bfloat16 [1536, 32768], P(None, ('dp', 'latent'))
- dec_grad: bfloat16 [32768, 1536], P(('dp', 'latent'))
- enc_bias_grad: float32 [32768], P(('dp', 'latent'))
- dec_bias_grad: float32 [1536], replicated
- mean_error: float32 [], replicated
Inputs may be any that keep to these rules, and one draw needn't show every extreme that they name: `slot_count`: slot lists of one device never repeat a (token block, latent block) pair among its 32 slots; entries past a device's count name valid blocks and are ignored; some device has all 32 slots live in every draw.
All inputs are finite; a program needn't handle non-finite values.
Results may differ from a plain program's by a relative error of at most 0.0065.
Values may be sent and summed in bfloat16 or wider, within the bound.
A program may use at most 128 MiB of HBM per device.

v0:
```python
import jax
import jax.numpy as jnp
from jax import lax
from jax.sharding import PartitionSpec as P

BLK = 128


def local(tokens, enc_weight, enc_bias, dec_weight, dec_bias, slot_token, slot_latent, slot_count):
    block_size = BLK
    gathered = lax.all_gather(tokens, "dp", axis=0, tiled=True)
    total_rows = gathered.shape[0]
    features = tokens.shape[1]
    capacity = slot_token.shape[0]
    live_count = slot_count[0]

    def forward_slot(slot_index, carried):
        activations, partial_value = carried
        row_start = slot_token[slot_index] * block_size
        col_start = slot_latent[slot_index] * block_size
        tok_rows = lax.dynamic_slice_in_dim(gathered, row_start, block_size, 0)
        enc_block = lax.dynamic_slice_in_dim(enc_weight, col_start, block_size, 1)
        bias_block = lax.dynamic_slice_in_dim(enc_bias, col_start, block_size, 0)
        active = (
            jnp.dot(tok_rows, enc_block, preferred_element_type=jnp.float32) + bias_block[None, :]
        ).astype(jnp.bfloat16)
        dec_block = lax.dynamic_slice_in_dim(dec_weight, col_start, block_size, 0)
        contrib = jnp.dot(active, dec_block, preferred_element_type=jnp.float32)
        previous = lax.dynamic_slice_in_dim(partial_value, row_start, block_size, 0)
        partial_value = lax.dynamic_update_slice_in_dim(
            partial_value, previous + contrib, row_start, 0
        )
        activations = lax.dynamic_update_index_in_dim(activations, active, slot_index, 0)
        return (activations, partial_value)

    empty_acts = jnp.zeros((capacity, block_size, block_size), jnp.bfloat16)
    empty_sum = jnp.zeros((total_rows, features), jnp.float32)
    activations, partial_value = lax.fori_loop(0, live_count, forward_slot, (empty_acts, empty_sum))
    share = lax.psum_scatter(partial_value, ("dp", "latent"), scatter_dimension=0, tiled=True)
    share_rows = share.shape[0]
    offset = lax.axis_index("latent") * share_rows
    token_share = lax.dynamic_slice_in_dim(tokens, offset, share_rows, 0)
    residual = share + dec_bias[None, :] - token_share.astype(jnp.float32)
    scaled = residual * 0.25
    squared, dec_bias_grad = lax.psum(
        (jnp.sum(residual * residual), jnp.sum(scaled, axis=0)), ("dp", "latent")
    )
    grad_all = lax.all_gather(scaled.astype(jnp.bfloat16), ("dp", "latent"), axis=0, tiled=True)
    mean_error = squared / (total_rows * features)

    def backward_slot(slot_index, gradients):
        enc_acc, dec_acc, bias_acc = gradients
        row_start = slot_token[slot_index] * block_size
        col_start = slot_latent[slot_index] * block_size
        tok_rows = lax.dynamic_slice_in_dim(gathered, row_start, block_size, 0)
        grad_block = lax.dynamic_slice_in_dim(grad_all, row_start, block_size, 0)
        dec_block = lax.dynamic_slice_in_dim(dec_weight, col_start, block_size, 0)
        pre_grad = lax.dot_general(
            grad_block, dec_block, (((1,), (1,)), ((), ())), preferred_element_type=jnp.float32
        )
        old_bias = lax.dynamic_slice_in_dim(bias_acc, col_start, block_size, 0)
        bias_acc = lax.dynamic_update_slice_in_dim(
            bias_acc, old_bias + jnp.sum(pre_grad, axis=0), col_start, 0
        )
        pre_half = pre_grad.astype(jnp.bfloat16)
        enc_term = lax.dot_general(
            tok_rows, pre_half, (((0,), (0,)), ((), ())), preferred_element_type=jnp.float32
        )
        old_enc = lax.dynamic_slice_in_dim(enc_acc, col_start, block_size, 1)
        enc_acc = lax.dynamic_update_slice_in_dim(enc_acc, old_enc + enc_term, col_start, 1)
        dec_term = lax.dot_general(
            activations[slot_index],
            grad_block,
            (((0,), (0,)), ((), ())),
            preferred_element_type=jnp.float32,
        )
        old_dec = lax.dynamic_slice_in_dim(dec_acc, col_start, block_size, 0)
        dec_acc = lax.dynamic_update_slice_in_dim(dec_acc, old_dec + dec_term, col_start, 0)
        return (enc_acc, dec_acc, bias_acc)

    latents_here = enc_weight.shape[1]
    start_grads = (
        jnp.zeros((features, latents_here), jnp.float32),
        jnp.zeros((latents_here, features), jnp.float32),
        jnp.zeros((latents_here,), jnp.float32),
    )
    enc_acc, dec_acc, bias_acc = lax.fori_loop(0, live_count, backward_slot, start_grads)
    return (
        enc_acc.astype(jnp.bfloat16),
        dec_acc.astype(jnp.bfloat16),
        bias_acc,
        dec_bias_grad,
        mean_error,
    )


def solution(mesh):
    in_specs = (
        P("dp", None),
        P(None, ("dp", "latent")),
        P(("dp", "latent")),
        P(("dp", "latent"), None),
        P(),
        P(("dp", "latent")),
        P(("dp", "latent")),
        P(("dp", "latent")),
    )
    out_specs = (
        P(None, ("dp", "latent")),
        P(("dp", "latent"), None),
        P(("dp", "latent")),
        P(),
        P(),
    )
    return jax.shard_map(local, mesh=mesh, in_specs=in_specs, out_specs=out_specs, check_vma=False)
```

profile of v0, /device:TPU:7, one launch (start us, length us, event | category | flops | bytes accessed | tf_op | source)
XLA Modules:
  0.0 829.1 jit_solution(1080155368049432398)
XLA Ops:
  8.0 60.8 %all-gather.3.cloned.1.call-done = bf16[1024,1536]{1,0:T(8,128)(2,1)} async-done(((bf16[128,1536]{1,0:T(8,128)(2,1)}), bf16[1024,1536]{1,0:T(8,128)(2,1)}) %all-gather.3.cloned.1.call-update) | async-done | bytes 3145744 | tf_op jit(solution)/shard_map/all_gather | solution.py:11
  69.0 3.4 broadcast.5.clone
  72.4 247.6 %while.26 = (s32[]{:T(128)}, bf16[32,128,128]{2,1,0:T(8,128)(2,1)S(1)}, f32[1024,1536]{1,0:T(8,128)}, s32[]{:T(128)}, s32[32]{0:T(128)S(1)}, /*index=5*/bf16[102...) while((s32[]{:T(128)}, ...), condition=%wide.region_1.2_spmd, body=%wide.region_0.1_spmd.sunk | while | flops 100892688 | bytes 2852675 | solution.py:38
  320.1 114.0 %reduce-scatter.2.cloned.1.call-done = f32[32,1536]{1,0:T(8,128)} async-done(((f32[1024,1536]{1,0:T(8,128)}), f32[32,1536]{1,0:T(8,128)}) %reduce-scatter.2.cloned.1.call-update) | async-done | bytes 196624 | tf_op jit(solution)/shard_map/reduce_scatter | solution.py:39
  436.3 41.5 %all-reduce = (f32[1536]{0:T(1024)}, f32[]{:T(128)}) all-reduce(f32[1536]{0:T(1024)S(1)} %get-tuple-element.125, f32[]{:T(128)} %get-tuple-element.124), channel_id=1, replica_groups=mesh['dp'=8,'latent'=4] {'dp','latent'}, use_global_device_ids=true, to_apply=%region_7.8 | all-reduce | flops 1537 | bytes 12296 | tf_op jit(solution)/shard_map/psum | solution.py:45
  478.5 18.6 %all-gather.5.cloned.1.call-done = bf16[1024,1536]{1,0:T(8,128)(2,1)} async-done(((bf16[32,1536]{1,0:T(8,128)(2,1)}), bf16[1024,1536]{1,0:T(8,128)(2,1)}) %all-gather.5.cloned.1.call-update) | async-done | bytes 3145744 | tf_op jit(solution)/shard_map/all_gather | solution.py:48
  497.2 3.4 broadcast.5
  500.6 3.4 broadcast_in_dim.15
  504.0 310.2 %while.27 = (s32[]{:T(128)}, f32[1536,1024]{1,0:T(8,128)}, f32[1024,1536]{1,0:T(8,128)}, f32[1024]{0:T(1024)S(1)}, s32[]{:T(128)}, /*index=5*/s32[32]{0:T(128)S(...) while((s32[]{:T(128)}, f32[1536,1024]{1,0:T(8,128)}, ...), condition=%wide.region_5.6_spmd, body=%wide.region_3.0_spmd.sunk | while | flops 151420944 | bytes 4819283 | solution.py:87
  508.8 2.5 fusion.41
  511.3 2.5 fusion.42
  518.5 2.5 fusion.41
  528.2 2.5 fusion.41
  537.9 2.5 fusion.41
  550.0 2.5 fusion.42
  557.3 2.5 fusion.41
  559.8 2.5 fusion.42
  567.0 2.5 fusion.41
  605.7 2.5 fusion.41
  634.7 2.5 fusion.41
  644.3 2.5 fusion.41
  654.0 2.5 fusion.41
  663.6 2.5 fusion.41
  673.3 2.5 fusion.41
  695.1 2.5 fusion.42
  702.4 2.5 fusion.41
  724.1 2.5 fusion.42
  741.1 2.5 fusion.41
  750.7 2.5 fusion.41
  779.7 2.5 fusion.41
  789.4 2.5 fusion.41
  814.3 5.1 convert_element_type.20
  (350 shorter events, 379.8 us)
Async XLA Ops:
  7.2 65.2 %copy-start.3 = (s32[32]{0:T(128)S(1)}, s32[32]{0:T(128)}, u32[]{:S(2)}) copy-start(s32[32]{0:T(128)} %param.18) | copy-start | bytes 388
  7.2 65.2 %copy-start.4 = (s32[32]{0:T(128)S(1)}, s32[32]{0:T(128)}, u32[]{:S(2)}) copy-start(s32[32]{0:T(128)} %param.17) | copy-start | bytes 388
  7.2 61.5 %all-gather.3.cloned.1.call-start = ((), (), s32[]{:S(2)}) async-start(), calls=%async_computation.1 | async-start | bytes 3538944 | tf_op jit(solution)/shard_map/all_gather | solution.py:11
  7.9 426.1 %reduce-scatter.2.cloned.1.call-start = ((), (), s32[]{:S(2)}) async-start(), calls=%async_computation.2 | async-start | bytes 6488064 | tf_op jit(solution)/shard_map/reduce_scatter | solution.py:39
  320.0 114.1 %copy-start.2 = (f32[1536]{0:T(1024)S(1)}, f32[1536]{0:T(1024)}, u32[]{:S(2)}) copy-start(f32[1536]{0:T(1024)} %param.16) | copy-start | bytes 18436
  320.0 177.2 %all-gather.5.cloned.1.call-start = ((), (), s32[]{:S(2)}) async-start(), calls=%async_computation.3 | async-start | bytes 3244032 | tf_op jit(solution)/shard_map/all_gather | solution.py:48
  814.2 7.2 copy-start.1
  814.3 5.1 copy-start
Sparse Core Ops, SparseCore 0:
  10.2 58.5 all-gather.2
  320.1 113.8 reduce-scatter.1
  437.5 59.6 all-gather.4
where the time goes:
time: 836 us; the launch traced here: 829 us
  matrix products  324 us (39%)
  waiting for transfers between devices  194 us (23%)
  loops' own time  128 us (15%)
  local copies, waits for them, and re-layouts  110 us (13%)
  blocking collectives  41.5 us (5%)
  between operations  15.6 us (2%)
  other arithmetic  15.4 us (2%)
    reduce_scatter x1, waiting for transfers between devices, local(): lax.psum_scatter(partial_value, ('dp', 'latent'), scatter_dimension=0, ti...  114 us
    dot_general x32, matrix products, backward_slot(): lax.dot_general(tok_rows, pre_half, (((0,), (0,)), ((), ())), preferred_e...  79.5 us
    dot_general x32, matrix products, backward_slot(): lax.dot_general(activations[slot_index], grad_block, (((0,), (0,)), ((),...  78.3 us
    dot_general x32, matrix products, forward_slot(): contrib = jnp.dot(active, dec_block, preferred_element_type=jnp.float32)  77.1 us
    another operation x1, loops' own time, local(): lax.fori_loop(0, live_count, backward_slot, start_grads)  64.1 us
    another operation x1, loops' own time, local(): lax.fori_loop(0, live_count, forward_slot, (empty_acts, empty_sum))  64.1 us
    all_gather x1, waiting for transfers between devices, local(): gathered = lax.all_gather(tokens, 'dp', axis=0, tiled=True)  60.8 us
    dot_general x32, matrix products, backward_slot(): lax.dot_general(grad_block, dec_block, (((1,), (1,)), ((), ())), preferre...  44.6 us
  transfers between devices with their start and end apart: 3, of which 3 were waited for; matrix products, arithmetic and copies ran while one was open for 0% of the time, Pallas kernels for 0%

commit v1 on v0

--- a/solution.py
+++ b/solution.py
@@ -6,9 +6,27 @@
 BLK = 128
 
 
+def joined_along(parts, dim):
+    shape = list(parts.shape[1:])
+    shape[dim] *= parts.shape[0]
+    return jnp.moveaxis(parts, 0, dim).reshape(shape)
+
+
+def collected_by_bits(value, axis):
+    count = lax.axis_size(axis)
+    pieces = value[None]
+    for level in range(count.bit_length() - 1):
+        bit = 1 << level
+        other = lax.ppermute(pieces, axis, [(i, i ^ bit) for i in range(count)])
+        both = jnp.stack([pieces, other])
+        upper = lax.axis_index(axis) >> level & 1
+        pieces = jnp.where(upper == 0, both, both[::-1]).reshape(-1, *value.shape)
+    return pieces
+
+
 def local(tokens, enc_weight, enc_bias, dec_weight, dec_bias, slot_token, slot_latent, slot_count):
     block_size = BLK
-    gathered = lax.all_gather(tokens, "dp", axis=0, tiled=True)
+    gathered = joined_along(collected_by_bits(tokens, "dp"), 0)
     total_rows = gathered.shape[0]
     features = tokens.shape[1]
     capacity = slot_token.shape[0]

time: 836 us -> 889 us (1.063)
  waiting for transfers between devices: 194 us -> 226 us
  matrix products: 324 us -> 336 us
    ppermute x0 -> x3, waiting for transfers between devices: none -> 93.8 us  [collected_by_bits(): other = lax.ppermute(pieces, axis, [(i, i ^ bit) for i in range(count)])]
    all_gather x1 -> x0, waiting for transfers between devices: 60.8 us -> none  [local(): gathered = lax.all_gather(tokens, 'dp', axis=0, tiled=True)]
    dot_general x32, matrix products: 44.2 us -> 59.7 us  [forward_slot(): jnp.dot(tok_rows, enc_block, preferred_element_type=jnp.float32)]
  transfers between devices with their start and end apart: 3 -> 5, of which waited for: 3 -> 5; matrix products, arithmetic and copies ran while one was open for 0% -> 0% of each run, Pallas kernels for 0% -> 0%
where the time goes in v1:
time: 889 us; the launch traced here: 881 us
  matrix products  336 us (38%)
  waiting for transfers between devices  226 us (25%)
  loops' own time  128 us (14%)
  local copies, waits for them, and re-layouts  111 us (12%)
  blocking collectives  41.6 us (5%)
  other arithmetic  17.9 us (2%)
  between operations  15.9 us (2%)
    reduce_scatter x1, waiting for transfers between devices, local(): lax.psum_scatter(partial_value, ('dp', 'latent'), scatter_dimension=0, ti...  113 us
    ppermute x3, waiting for transfers between devices, collected_by_bits(): other = lax.ppermute(pieces, axis, [(i, i ^ bit) for i in range(count)])  93.8 us
    dot_general x32, matrix products, backward_slot(): lax.dot_general(activations[slot_index], grad_block, (((0,), (0,)), ((),...  79.1 us
    dot_general x32, matrix products, forward_slot(): contrib = jnp.dot(active, dec_block, preferred_element_type=jnp.float32)  76.9 us
    dot_general x32, matrix products, backward_slot(): lax.dot_general(tok_rows, pre_half, (((0,), (0,)), ((), ())), preferred_e...  76 us
    another operation x1, loops' own time, local(): lax.fori_loop(0, live_count, backward_slot, start_grads)  64.1 us
    another operation x1, loops' own time, local(): lax.fori_loop(0, live_count, forward_slot, (empty_acts, empty_sum))  64.1 us
    dot_general x32, matrix products, forward_slot(): jnp.dot(tok_rows, enc_block, preferred_element_type=jnp.float32)  59.7 us
  transfers between devices with their start and end apart: 5, of which 5 were waited for; matrix products, arithmetic and copies ran while one was open for 0% of the time, Pallas kernels for 0%

profile of v1, /device:TPU:7, one launch (start us, length us, event | category | flops | bytes accessed | tf_op | source)
XLA Modules:
  0.0 881.0 jit_solution(8619268157678724345)
XLA Ops:
  7.5 10.0 %collective-permute-done = bf16[1,128,1536]{2,1,0:T(8,128)(2,1)S(1)} collective-permute-done((bf16[1,128,1536]{2,1,0:T(8,128)(2,1)}, bf16[1,128,1536]{2,1,0:T(8,128)(2,1)S(1)}, u32[]{:S(2)}, u32[]{:S(2)}) %collective-permute-start) | collective-permute-done | bytes 393248 | tf_op jit(solution)/shard_map/ppermute | solution.py:20
  20.1 16.3 %collective-permute-done.1 = bf16[2,128,1536]{2,1,0:T(8,128)(2,1)S(1)} collective-permute-done((bf16[2,128,1536]{2,1,0:T(8,128)(2,1)S(1)}, bf16[2,128,1536]{2,1,0:T(8,128)(2,1)S(1)}, u32[]{:S(2)}, u32[]{:S(2)}) %collective-permute-start.1) | collective-permute-done | bytes 786464 | tf_op jit(solution)/shard_map/ppermute | solution.py:20
  39.2 67.6 %collective-permute-done.2 = bf16[4,128,1536]{2,1,0:T(8,128)(2,1)S(1)} collective-permute-done((bf16[4,128,1536]{2,1,0:T(8,128)(2,1)S(1)}, bf16[4,128,1536]{2,1,0:T(8,128)(2,1)S(1)}, u32[]{:S(2)}, u32[]{:S(2)}) %collective-permute-start.2) | collective-permute-done | bytes 1572896 | tf_op jit(solution)/shard_map/ppermute | solution.py:20
  108.9 3.5 broadcast.5.clone
  112.4 262.7 %while.26 = (s32[]{:T(128)}, bf16[32,128,128]{2,1,0:T(8,128)(2,1)}, f32[1024,1536]{1,0:T(8,128)}, s32[]{:T(128)}, s32[32]{0:T(128)S(1)}, /*index=5*/bf16[1024,15...) while((s32[]{:T(128)}, bf16[32,128,128]{2,1,0:T(8,128)(2,1)}, ...), condition=%wide.region_1.2_spmd, body=%wide.region_0.1_spmd.sunk | while | flops 100892688 | bytes 2852675 | solution.py:56
  375.2 113.1 %reduce-scatter.2.cloned.1.call-done = f32[32,1536]{1,0:T(8,128)} async-done(((f32[1024,1536]{1,0:T(8,128)}), f32[32,1536]{1,0:T(8,128)}) %reduce-scatter.2.cloned.1.call-update) | async-done | bytes 196624 | tf_op jit(solution)/shard_map/reduce_scatter | solution.py:57
  490.6 41.6 %all-reduce = (f32[1536]{0:T(1024)}, f32[]{:T(128)}) all-reduce(f32[1536]{0:T(1024)S(1)} %get-tuple-element.125, f32[]{:T(128)} %get-tuple-element.124), channel_id=1, replica_groups=mesh['dp'=8,'latent'=4] {'dp','latent'}, use_global_device_ids=true, to_apply=%region_7.8 | all-reduce | flops 1537 | bytes 12296 | tf_op jit(solution)/shard_map/psum | solution.py:63
  532.8 18.6 %all-gather.2.cloned.1.call-done = bf16[1024,1536]{1,0:T(8,128)(2,1)} async-done(((bf16[32,1536]{1,0:T(8,128)(2,1)}), bf16[1024,1536]{1,0:T(8,128)(2,1)}) %all-gather.2.cloned.1.call-update) | async-done | bytes 3145744 | tf_op jit(solution)/shard_map/all_gather | solution.py:66
  551.5 3.4 broadcast.5
  554.9 3.5 broadcast_in_dim.18
  558.4 307.5 %while.27 = (s32[]{:T(128)}, f32[1536,1024]{1,0:T(8,128)}, f32[1024,1536]{1,0:T(8,128)}, f32[1024]{0:T(1024)S(1)}, s32[]{:T(128)}, /*index=5*/s32[32]{0:T(128)S(...) while((s32[]{:T(128)}, f32[1536,1024]{1,0:T(8,128)}, ...), condition=%wide.region_5.6_spmd, body=%wide.region_3.5_spmd.sunk | while | flops 151420944 | bytes 4819283 | solution.py:105
  565.4 2.5 fusion.44
  584.6 2.5 fusion.44
  603.7 2.5 fusion.44
  613.3 2.5 fusion.44
  632.5 2.5 fusion.44
  642.1 2.5 fusion.44
  651.8 2.5 fusion.44
  670.9 2.5 fusion.44
  680.6 2.5 fusion.44
  718.8 2.5 fusion.44
  728.4 2.5 fusion.44
  738.0 2.5 fusion.44
  747.6 2.5 fusion.44
  766.8 2.5 fusion.44
  776.4 2.5 fusion.44
  786.0 2.5 fusion.44
  814.8 2.5 fusion.44
  824.4 2.5 fusion.44
  853.1 2.5 fusion.44
  862.7 2.5 fusion.44
  865.9 5.1 convert_element_type.20
  (359 shorter events, 404.5 us)
Async XLA Ops:
  7.2 481.2 %reduce-scatter.2.cloned.1.call-start = ((), (), s32[]{:S(2)}) async-start(), calls=%async_computation.1 | async-start | bytes 6488064 | tf_op jit(solution)/shard_map/reduce_scatter | solution.py:57
  7.2 10.3 %collective-permute-start = (bf16[1,128,1536]{2,1,0:T(8,128)(2,1)}, bf16[1,128,1536]{2,1,0:T(8,128)(2,1)S(1)}, u32[]{:S(2)}, u32[]{:S(2)}) collective-permute-start(bf16[1,128,1536]{2,1,0:T(8,128)(2,1)} %bitcast.45), channel_id=1, source_target_pairs={{0,4},{4,0},{8,12},{12,8},{16,20},{20,16},{24,28},{28,24},{1,5},{5... | collective-permute-start | bytes 1179656 | tf_op jit(solution)/shard_map/ppermute | solution.py:20
  18.7 17.6 %collective-permute-start.1 = (bf16[2,128,1536]{2,1,0:T(8,128)(2,1)S(1)}, bf16[2,128,1536]{2,1,0:T(8,128)(2,1)S(1)}, u32[]{:S(2)}, u32[]{:S(2)}) collective-permute-start(bf16[2,128,1536]{2,1,0:T(8,128)(2,1)S(1)} %get-tuple-element.175), channel_id=1, source_target_pairs={{0,8},{4,12},{8,0},{12,4},{16,24},{20,28},{24,16},{28,20},{1,9},{5... | collective-permute-start | bytes 2359304 | tf_op jit(solution)/shard_map/ppermute | solution.py:20
  36.8 70.0 %collective-permute-start.2 = (bf16[4,128,1536]{2,1,0:T(8,128)(2,1)S(1)}, bf16[4,128,1536]{2,1,0:T(8,128)(2,1)S(1)}, u32[]{:S(2)}, u32[]{:S(2)}) collective-permute-start(bf16[4,128,1536]{2,1,0:T(8,128)(2,1)S(1)} %bitcast.41), channel_id=1, source_target_pairs={{0,16},{4,20},{8,24},{12,28},{16,0},{20,4},{24,8},{28,12},{1,17},{... | collective-permute-start | bytes 4718600 | tf_op jit(solution)/shard_map/ppermute | solution.py:20
  108.9 3.5 copy-start.3
  108.9 3.5 copy-start.4
  375.1 113.2 %copy-start.2 = (f32[1536]{0:T(1024)S(1)}, f32[1536]{0:T(1024)}, u32[]{:S(2)}) copy-start(f32[1536]{0:T(1024)} %param.16) | copy-start | bytes 18436
  375.2 176.3 %all-gather.2.cloned.1.call-start = ((), (), s32[]{:S(2)}) async-start(), calls=%async_computation.2 | async-start | bytes 3244032 | tf_op jit(solution)/shard_map/all_gather | solution.py:66
  865.8 5.1 copy-start.1
  865.9 5.1 copy-start
Sparse Core Ops, SparseCore 0:
  375.3 113.0 reduce-scatter.1
  491.8 59.6 all-gather.1
